TPU v7x, 512 devices: a whole 4x8x8 slice. The times are simulated.
512 devices in a mesh: chain: 64 (over y, x, core), cols: 8 (over z).
Axes of the slice: x: 4, y: 8, z: 8, core: 2. Of those that a mesh axis runs over, the one named last changes fastest.
Arguments:
- start_vectors: float32 [1024, 256, 256], P('chain', 'cols'), may hold values from -6 to 6
- factors: float32 [1024, 256, 256], P('chain', 'cols'), may hold values from -1.2 to 1.2, as said below
Outputs:
- vectors: float32 [1024, 256, 256], P('chain', 'cols')
- log_growth: float32 [256], P('cols')
Inputs may be any that keep to these rules, and one draw needn't show every extreme that they name: `factors`: the factor blocks of the shifted operator; every product of consecutive factor blocks is bounded.
All inputs are finite; a program needn't handle non-finite values.
Results may differ from a plain program's by a relative error of at most 0.0003.
Values sent between devices are 32-bit elements; how exact they have to be, the bound alone decides.
No kernel may reach another device: no remote copies, remote signals or barrier semaphores. Data moves between devices by JAX's collectives and lax.ppermute only.
A program may use at most 128 MiB of HBM per device.

v0:
```python
import jax
import jax.numpy as jnp
from jax import lax
from jax.sharding import PartitionSpec as P

eps_value = 1e-06


def from_behind(block, axis, distance):
    devices = range(lax.axis_size(axis))
    route = [(i - distance, i) for i in devices if i - distance in devices]
    return lax.ppermute(block, axis, route)


def transform(matrix, vectors_in):
    return lax.dot_general(
        vectors_in,
        matrix,
        (((1,), (1,)), ((), ())),
        precision=lax.Precision.HIGHEST,
        preferred_element_type=jnp.float32,
    )


def compose(later, earlier):
    return jnp.dot(
        later, earlier, precision=lax.Precision.HIGHEST, preferred_element_type=jnp.float32
    )


def forward_rows(factors, right_side, incoming):

    def forward_advance(carried, element):
        matrix, source = element
        carried = transform(matrix, carried) + source
        return (carried, carried)

    return lax.scan(forward_advance, incoming, (factors, right_side))


def backward_rows(factors, forward, incoming):

    def backward_advance(carried, element):
        matrix, source = element
        carried = transform(matrix, source + carried)
        return (carried, carried)

    return lax.scan(backward_advance, incoming, (factors, forward), reverse=True)


def chain_operator(factors, reverse):
    identity_block = jnp.eye(factors.shape[1], dtype=jnp.float32)

    def chain_advance(running, matrix):
        return (compose(matrix, running), None)

    running, _ = lax.scan(chain_advance, identity_block, factors, reverse=reverse)
    return running


def section_count():
    return (lax.axis_size("chain") - 1).bit_length()


def enter_state(summary, direction):
    return from_behind(summary, "chain", direction)


def solve_system(factors, right_side, prefix_forward, prefix_backward):
    zero_state = jnp.zeros(right_side.shape[1:], jnp.float32)
    local_last, _ = forward_rows(factors, right_side, zero_state)
    incoming = enter_state(prefix_forward(local_last), 1)
    _, forward = forward_rows(factors, right_side, incoming)
    local_first, _ = backward_rows(factors, forward, zero_state)
    incoming_back = enter_state(prefix_backward(local_first), -1)
    _, solved = backward_rows(factors, forward, incoming_back)
    return solved


def shards(start_vectors, factors):
    full_factors = lax.all_gather(factors, "cols", axis=1, tiled=True)

    def pair_prefix(operator, summary, direction):
        sections = section_count()
        for section_index in range(sections):
            distance = direction * (1 << section_index)
            if section_index + 1 < sections:
                received_op, received_sum = from_behind((operator, summary), "chain", distance)
                summary = transform(operator, received_sum) + summary
                operator = compose(operator, received_op)
            else:
                received_sum = from_behind(summary, "chain", distance)
                summary = transform(operator, received_sum) + summary
        return summary

    def prefix_forward(summary):
        return pair_prefix(chain_operator(full_factors, False), summary, 1)

    def prefix_backward(summary):
        return pair_prefix(chain_operator(full_factors, True), summary, -1)

    cell_count = start_vectors.shape[0] * lax.axis_size("chain") * start_vectors.shape[2]
    first_solve = solve_system(full_factors, start_vectors, prefix_forward, prefix_backward)
    first_squares = lax.psum(jnp.sum(first_solve * first_solve, axis=(0, 2)), "chain")
    scale_one = jnp.sqrt(first_squares / cell_count + eps_value)
    second_solve = solve_system(
        full_factors, first_solve / scale_one[None, :, None], prefix_forward, prefix_backward
    )
    second_squares = lax.psum(jnp.sum(second_solve * second_solve, axis=(0, 2)), "chain")
    scale_two = jnp.sqrt(second_squares / cell_count + eps_value)
    result_vectors = second_solve / scale_two[None, :, None]
    return (result_vectors, jnp.log(scale_two))


def solution(mesh):
    return jax.shard_map(
        shards,
        mesh=mesh,
        in_specs=(P("chain", "cols", None), P("chain", "cols", None)),
        out_specs=(P("chain", "cols", None), P("cols")),
        check_vma=False,
    )
```

profile of v0, /device:TPU:32, one launch (start us, length us, event | category | flops | bytes accessed | tf_op | source)
XLA Modules:
  0.0 812.4 jit_solution(6026892274242298097)
XLA Ops:
  8.0 64.7 %all-gather.2.cloned.1.call-done = f32[16,256,256]{2,1,0:T(8,128)} async-done(((f32[16,32,256]{2,1,0:T(8,128)}), f32[16,256,256]{2,1,0:T(8,128)}) %all-gather.2.cloned.1.call-update) | async-done | bytes 4194320 | tf_op jit(solution)/shard_map/all_gather | solution.py:81
  72.7 21.4 %while.146 = (s32[]{:T(128)}, f32[32,256]{1,0:T(8,128)S(1)}, f32[16,256,256]{2,1,0:T(8,128)}, f32[16,32,256]{2,1,0:T(8,128)}, s32[]{:T(128)}, /*index=5*/s32[]{:T(128)}) while((s32[]{:T(128)}, f32[32,256]{1,0:T(8,128)S(1)}, f32[16,256,256]{2,1,0:T(8,128)}, f32[16,32,256]{2,1,0:T(8,128)}, s32[]{:T(128)}, /*index=5*/s32[]{:T(128)}) %tuple.241), condition=%wide.region_1.2_spmd.clone, body=%wide.region_0.1_spmd.clone.sunk | while | flops 25182212 | bytes 427087 | solution.py:38
  96.0 22.1 %while.138 = (s32[]{:T(128)}, f32[256,256]{1,0:T(8,128)S(1)}, f32[16,256,256]{2,1,0:T(8,128)}, s32[]{:T(128)}) while((s32[]{:T(128)}, f32[256,256]{1,0:T(8,128)S(1)}, f32[16,256,256]{2,1,0:T(8,128)}, s32[]{:T(128)}) %tuple.273), condition=%wide.region_3.4_spmd, body=%wide.region_2.3_spmd.sunk | while | flops 201326592 | bytes 1311285 | solution.py:57
  134.6 7.3 collective-permute-done.4
  146.4 10.8 %collective-permute-done.6 = f32[256,256]{1,0:T(8,128)S(1)} collective-permute-done((f32[256,256]{1,0:T(8,128)S(1)}, f32[256,256]{1,0:T(8,128)S(1)}, u32[]{:S(2)}, u32[]{:S(2)}) %collective-permute-start.6) | collective-permute-done | bytes 262176 | tf_op jit(solution)/shard_map/ppermute | solution.py:12
  161.9 7.5 collective-permute-done.8
  173.3 7.5 collective-permute-done.10
  184.0 6.6 collective-permute-done.11
  190.7 21.4 %while.139 = (s32[]{:T(128)}, f32[32,256]{1,0:T(8,128)S(1)}, f32[16,32,256]{2,1,0:T(8,128)S(1)}, f32[16,256,256]{2,1,0:T(8,128)}, f32[16,32,256]{2,1,0:T(8,128)}, /*index=5*/s32[]{:T(128)}) while((s32[]{:T(128)}, f32[32,256]{1,0:T(8,128)S(1)}, f32[16,32,256]{2,1,0:T(8,128)S(1)}, f32[16,256,256]{2,1,0:T(8,128)}, f32[16,32,256]{2,1,0:T(8,128)}, ...), condition=%wide.region_5.6_spmd, body=%wide.region_4.5_spmd.sunk | while | flops 25174016 | bytes 459845 | solution.py:38
  212.1 21.3 %while.140 = (s32[]{:T(128)}, f32[32,256]{1,0:T(8,128)S(1)}, f32[16,32,256]{2,1,0:T(8,128)S(1)}, f32[16,256,256]{2,1,0:T(8,128)}, s32[]{:T(128)}, /*index=5*/s32[]{:T(128)}) while((s32[]{:T(128)}, f32[32,256]{1,0:T(8,128)S(1)}, f32[16,32,256]{2,1,0:T(8,128)S(1)}, f32[16,256,256]{2,1,0:T(8,128)}, s32[]{:T(128)}, /*index=5*/s32[]{:T(128)}) %tuple.275), condition=%wide.region_7.8_spmd, body=%wide.region_6.7_spmd.sunk | while | flops 25174020 | bytes 427089 | solution.py:48
  235.4 22.1 %while.141 = (s32[]{:T(128)}, f32[256,256]{1,0:T(8,128)S(1)}, f32[16,256,256]{2,1,0:T(8,128)}, s32[]{:T(128)}, s32[]{:T(128)}) while((s32[]{:T(128)}, f32[256,256]{1,0:T(8,128)S(1)}, f32[16,256,256]{2,1,0:T(8,128)}, s32[]{:T(128)}, s32[]{:T(128)}) %tuple.276), condition=%wide.region_9.10_spmd, body=%wide.region_8.9_spmd.sunk | while | flops 201326592 | bytes 1310797 | solution.py:57
  278.5 7.5 collective-permute-done.18
  290.7 6.7 collective-permute-done.20
  301.4 13.4 %collective-permute-done.22 = f32[256,256]{1,0:T(8,128)S(1)} collective-permute-done((f32[256,256]{1,0:T(8,128)S(1)}, f32[256,256]{1,0:T(8,128)S(1)}, u32[]{:S(2)}, u32[]{:S(2)}) %collective-permute-start.22) | collective-permute-done | bytes 262176 | tf_op jit(solution)/shard_map/ppermute | solution.py:12
  315.6 5.5 collective-permute-start.23
  322.7 21.6 %while.142 = (s32[]{:T(128)}, f32[32,256]{1,0:T(8,128)S(1)}, f32[16,32,256]{2,1,0:T(8,128)S(1)}, f32[16,32,256]{2,1,0:T(8,128)}, f32[16,256,256]{2,1,0:T(8,128)}, /*index=5*/s32[]{:T(128)}, s32[]{:T(128)}) while((s32[]{:T(128)}, f32[32,256]{1,0:T(8,128)S(1)}, f32[16,32,256]{2,1,0:T(8,128)S(1)}, f32[16,32,256]{2,1,0:T(8,128)}, ...), condition=%wide.region_11.12_spmd, body=%wide.region_10.11_spmd.sunk | while | flops 25174020 | bytes 460377 | solution.py:48
  344.5 129.1 %psum.14 = f32[32]{0:T(128)S(1)} all-reduce(f32[32]{0:T(128)S(1)} %multiply_reduce_fusion.1), channel_id=1, replica_groups=mesh['chain'=64,'cols'=8] {'chain'}, use_global_device_ids=true, to_apply=%region_13.14 | all-reduce | flops 32 | bytes 256 | tf_op jit(solution)/shard_map/psum | solution.py:104
  474.5 21.5 %while.147 = (s32[]{:T(128)}, f32[32,256]{1,0:T(8,128)S(1)}, f32[16,256,256]{2,1,0:T(8,128)}, f32[16,32,256]{2,1,0:T(8,128)}, s32[]{:T(128)}, /*index=5*/s32[]{:T(128)}) while((s32[]{:T(128)}, f32[32,256]{1,0:T(8,128)S(1)}, f32[16,256,256]{2,1,0:T(8,128)}, f32[16,32,256]{2,1,0:T(8,128)}, s32[]{:T(128)}, ...), condition=%wide.region_15.16_spmd.clone, body=%wide.region_14.15_spmd.clone.sunk | while | flops 25182212 | bytes 427087 | solution.py:38
  497.9 6.6 collective-permute-done.24
  506.8 7.2 collective-permute-done.25
  516.4 7.5 collective-permute-done.26
  526.2 5.1 collective-permute-done.27
  533.6 6.0 collective-permute-done.28
  541.4 8.2 %collective-permute-done.29 = f32[32,256]{1,0:T(8,128)S(1)} collective-permute-done((f32[32,256]{1,0:T(8,128)S(1)}, f32[32,256]{1,0:T(8,128)S(1)}, u32[]{:S(2)}, u32[]{:S(2)}) %collective-permute-start.29) | collective-permute-done | bytes 32800 | tf_op jit(solution)/shard_map/ppermute | solution.py:12
  551.9 6.6 collective-permute-done.30
  558.6 21.4 %while.143 = (s32[]{:T(128)}, f32[32,256]{1,0:T(8,128)S(1)}, f32[16,32,256]{2,1,0:T(8,128)S(1)}, f32[16,256,256]{2,1,0:T(8,128)}, f32[16,32,256]{2,1,0:T(8,128)}, /*index=5*/s32[]{:T(128)}) while((s32[]{:T(128)}, f32[32,256]{1,0:T(8,128)S(1)}, f32[16,32,256]{2,1,0:T(8,128)S(1)}, f32[16,256,256]{2,1,0:T(8,128)}, f32[16,32,256]{2,1,0:T(8,128)}, ...), condition=%wide.region_17.18_spmd, body=%wide.region_16.17_spmd.sunk | while | flops 25174016 | bytes 459845 | solution.py:38
  580.0 21.3 %while.144 = (s32[]{:T(128)}, f32[32,256]{1,0:T(8,128)S(1)}, f32[16,32,256]{2,1,0:T(8,128)S(1)}, f32[16,256,256]{2,1,0:T(8,128)}, s32[]{:T(128)}, /*index=5*/s32[]{:T(128)}) while((s32[]{:T(128)}, f32[32,256]{1,0:T(8,128)S(1)}, f32[16,32,256]{2,1,0:T(8,128)S(1)}, f32[16,256,256]{2,1,0:T(8,128)}, s32[]{:T(128)}, /*index=5*/s32[]{:T(128)}) %tuple.280), condition=%wide.region_19.20_spmd, body=%wide.region_18.19_spmd.sunk | while | flops 25174020 | bytes 427089 | solution.py:48
  613.3 5.4 collective-permute-done.33
  627.3 4.8 collective-permute-done.35
  635.6 16.2 %collective-permute-start.37 = (f32[32,256]{1,0:T(8,128)S(1)}, f32[32,256]{1,0:T(8,128)S(1)}, u32[]{:S(2)}, u32[]{:S(2)}) collective-permute-start(f32[32,256]{1,0:T(8,128)S(1)} %convolution_add_fusion), channel_id=1, source_target_pairs={{8,0},{16,8},{24,16},{32,24},{40,32},{48,40},{56,48},{64,56},{72,6... | collective-permute-start | bytes 98312 | tf_op jit(solution)/shard_map/ppermute | solution.py:12
  653.5 21.3 %while.145 = (s32[]{:T(128)}, f32[32,256]{1,0:T(8,128)S(1)}, f32[16,32,256]{2,1,0:T(8,128)S(1)}, f32[16,32,256]{2,1,0:T(8,128)S(1)}, f32[16,256,256]{2,1,0:T(8,128)}, /*index=5*/s32[]{:T(128)}, s32[]{:T(128)}) while((s32[]{:T(128)}, f32[32,256]{1,0:T(8,128)S(1)}, f32[16,32,256]{2,1,0:T(8,128)S(1)}, f32[16,32,256]{2,1,0:T(8,128)S(1)}, ...), condition=%wide.region_21.22_spmd, body=%wide.region_20.21_spmd.sunk | while | flops 25174020 | bytes 460377 | solution.py:48
  675.0 129.1 %psum.15 = f32[32]{0:T(128)S(1)} all-reduce(f32[32]{0:T(128)S(1)} %multiply_reduce_fusion), channel_id=1, replica_groups=mesh['chain'=64,'cols'=8] {'chain'}, use_global_device_ids=true, to_apply=%region_23.24 | all-reduce | flops 32 | bytes 256 | tf_op jit(solution)/shard_map/psum | solution.py:109
  (435 shorter events, 323.3 us)
Async XLA Ops:
  7.2 65.5 %all-gather.2.cloned.1.call-start = ((), (), s32[]{:S(2)}) async-start(), calls=%async_computation | async-start | bytes 4718592 | tf_op jit(solution)/shard_map/all_gather | solution.py:81
  94.1 27.5 %collective-permute-start = (f32[32,256]{1,0:T(8,128)S(1)}, f32[32,256]{1,0:T(8,128)S(1)}, u32[]{:S(2)}, u32[]{:S(2)}) collective-permute-start(f32[32,256]{1,0:T(8,128)S(1)} %get-tuple-element.568), channel_id=1, source_target_pairs={{0,8},{8,16},{16,24},{24,32},{32,40},{40,48},{48,56},{56,64},{64,7... | collective-permute-start | bytes 98312 | tf_op jit(solution)/shard_map/ppermute | solution.py:12
  118.1 11.0 %collective-permute-start.2 = (f32[256,256]{1,0:T(8,128)S(1)}, f32[256,256]{1,0:T(8,128)S(1)}, u32[]{:S(2)}, u32[]{:S(2)}) collective-permute-start(f32[256,256]{1,0:T(8,128)S(1)} %get-tuple-element.569), channel_id=1, source_target_pairs={{0,8},{8,16},{16,24},{24,32},{32,40},{40,48},{48,56},{56,64},{64,7... | collective-permute-start | bytes 786440 | tf_op jit(solution)/shard_map/ppermute | solution.py:12
  122.0 9.5 %collective-permute-start.1 = (f32[32,256]{1,0:T(8,128)S(1)}, f32[32,256]{1,0:T(8,128)S(1)}, u32[]{:S(2)}, u32[]{:S(2)}) collective-permute-start(f32[32,256]{1,0:T(8,128)S(1)} %convolution_add_fusion.23), channel_id=1, source_target_pairs={{0,16},{8,24},{16,32},{24,40},{32,48},{40,56},{48,64},{56,72},{64,... | collective-permute-start | bytes 98312 | tf_op jit(solution)/shard_map/ppermute | solution.py:12
  129.5 12.3 %collective-permute-start.4 = (f32[256,256]{1,0:T(8,128)S(1)}, f32[256,256]{1,0:T(8,128)S(1)}, u32[]{:S(2)}, u32[]{:S(2)}) collective-permute-start(f32[256,256]{1,0:T(8,128)S(1)} %fusion.54), channel_id=1, source_target_pairs={{0,16},{8,24},{16,32},{24,40},{32,48},{40,56},{48,64},{56,72},{64,... | collective-permute-start | bytes 786440 | tf_op jit(solution)/shard_map/ppermute | solution.py:12
  131.8 12.3 %collective-permute-start.3 = (f32[32,256]{1,0:T(8,128)S(1)}, f32[32,256]{1,0:T(8,128)S(1)}, u32[]{:S(2)}, u32[]{:S(2)}) collective-permute-start(f32[32,256]{1,0:T(8,128)S(1)} %convolution_add_fusion.22), channel_id=1, source_target_pairs={{0,32},{8,40},{16,48},{24,56},{32,64},{40,72},{48,80},{56,88},{64,... | collective-permute-start | bytes 98312 | tf_op jit(solution)/shard_map/ppermute | solution.py:12
  142.2 15.0 %collective-permute-start.6 = (f32[256,256]{1,0:T(8,128)S(1)}, f32[256,256]{1,0:T(8,128)S(1)}, u32[]{:S(2)}, u32[]{:S(2)}) collective-permute-start(f32[256,256]{1,0:T(8,128)S(1)} %fusion.55), channel_id=1, source_target_pairs={{0,32},{8,40},{16,48},{24,56},{32,64},{40,72},{48,80},{56,88},{64,... | collective-permute-start | bytes 786440 | tf_op jit(solution)/shard_map/ppermute | solution.py:12
  144.5 15.1 %collective-permute-start.5 = (f32[32,256]{1,0:T(8,128)S(1)}, f32[32,256]{1,0:T(8,128)S(1)}, u32[]{:S(2)}, u32[]{:S(2)}) collective-permute-start(f32[32,256]{1,0:T(8,128)S(1)} %convolution_add_fusion.21), channel_id=1, source_target_pairs={{0,64},{8,72},{16,80},{24,88},{32,96},{40,104},{48,112},{56,120},{... | collective-permute-start | bytes 98312 | tf_op jit(solution)/shard_map/ppermute | solution.py:12
  157.6 11.7 %collective-permute-start.8 = (f32[256,256]{1,0:T(8,128)S(1)}, f32[256,256]{1,0:T(8,128)S(1)}, u32[]{:S(2)}, u32[]{:S(2)}) collective-permute-start(f32[256,256]{1,0:T(8,128)S(1)} %fusion.56), channel_id=1, source_target_pairs={{0,64},{8,72},{16,80},{24,88},{32,96},{40,104},{48,112},{56,120},{... | collective-permute-start | bytes 786440 | tf_op jit(solution)/shard_map/ppermute | solution.py:12
  159.9 11.7 %collective-permute-start.7 = (f32[32,256]{1,0:T(8,128)S(1)}, f32[32,256]{1,0:T(8,128)S(1)}, u32[]{:S(2)}, u32[]{:S(2)}) collective-permute-start(f32[32,256]{1,0:T(8,128)S(1)} %convolution_add_fusion.20), channel_id=1, source_target_pairs={{0,128},{8,136},{16,144},{24,152},{32,160},{40,168},{48,176},{56,1... | collective-permute-start | bytes 98312 | tf_op jit(solution)/shard_map/ppermute | solution.py:12
  169.7 11.1 %collective-permute-start.10 = (f32[256,256]{1,0:T(8,128)S(1)}, f32[256,256]{1,0:T(8,128)S(1)}, u32[]{:S(2)}, u32[]{:S(2)}) collective-permute-start(f32[256,256]{1,0:T(8,128)S(1)} %fusion.57), channel_id=1, source_target_pairs={{0,128},{8,136},{16,144},{24,152},{32,160},{40,168},{48,176},{56,1... | collective-permute-start | bytes 786440 | tf_op jit(solution)/shard_map/ppermute | solution.py:12
  172.0 9.7 %collective-permute-start.9 = (f32[32,256]{1,0:T(8,128)S(1)}, f32[32,256]{1,0:T(8,128)S(1)}, u32[]{:S(2)}, u32[]{:S(2)}) collective-permute-start(f32[32,256]{1,0:T(8,128)S(1)} %convolution_add_fusion.19), channel_id=1, source_target_pairs={{0,256},{8,264},{16,272},{24,280},{32,288},{40,296},{48,304},{56,3... | collective-permute-start | bytes 98312 | tf_op jit(solution)/shard_map/ppermute | solution.py:12
  182.1 8.6 %collective-permute-start.11 = (f32[32,256]{1,0:T(8,128)S(1)}, f32[32,256]{1,0:T(8,128)S(1)}, u32[]{:S(2)}, u32[]{:S(2)}) collective-permute-start(f32[32,256]{1,0:T(8,128)S(1)} %convolution_add_fusion.18), channel_id=1, source_target_pairs={{0,8},{8,16},{16,24},{24,32},{32,40},{40,48},{48,56},{56,64},{64,7... | collective-permute-start | bytes 98312 | tf_op jit(solution)/shard_map/ppermute | solution.py:12
  233.5 26.0 %collective-permute-start.12 = (f32[32,256]{1,0:T(8,128)S(1)}, f32[32,256]{1,0:T(8,128)S(1)}, u32[]{:S(2)}, u32[]{:S(2)}) collective-permute-start(f32[32,256]{1,0:T(8,128)S(1)} %get-tuple-element.571), channel_id=1, source_target_pairs={{8,0},{16,8},{24,16},{32,24},{40,32},{48,40},{56,48},{64,56},{72,6... | collective-permute-start | bytes 98312 | tf_op jit(solution)/shard_map/ppermute | solution.py:12
  264.1 9.8 %collective-permute-start.16 = (f32[256,256]{1,0:T(8,128)S(1)}, f32[256,256]{1,0:T(8,128)S(1)}, u32[]{:S(2)}, u32[]{:S(2)}) collective-permute-start(f32[256,256]{1,0:T(8,128)S(1)} %fusion.59), channel_id=1, source_target_pairs={{16,0},{24,8},{32,16},{40,24},{48,32},{56,40},{64,48},{72,56},{80,... | collective-permute-start | bytes 786440 | tf_op jit(solution)/shard_map/ppermute | solution.py:12
  266.9 9.2 %collective-permute-start.15 = (f32[32,256]{1,0:T(8,128)S(1)}, f32[32,256]{1,0:T(8,128)S(1)}, u32[]{:S(2)}, u32[]{:S(2)}) collective-permute-start(f32[32,256]{1,0:T(8,128)S(1)} %convolution_add_fusion.16), channel_id=1, source_target_pairs={{32,0},{40,8},{48,16},{56,24},{64,32},{72,40},{80,48},{88,56},{96,... | collective-permute-start | bytes 98312 | tf_op jit(solution)/shard_map/ppermute | solution.py:12
  274.3 11.7 %collective-permute-start.18 = (f32[256,256]{1,0:T(8,128)S(1)}, f32[256,256]{1,0:T(8,128)S(1)}, u32[]{:S(2)}, u32[]{:S(2)}) collective-permute-start(f32[256,256]{1,0:T(8,128)S(1)} %fusion.60), channel_id=1, source_target_pairs={{32,0},{40,8},{48,16},{56,24},{64,32},{72,40},{80,48},{88,56},{96,... | collective-permute-start | bytes 786440 | tf_op jit(solution)/shard_map/ppermute | solution.py:12
  276.5 11.9 %collective-permute-start.17 = (f32[32,256]{1,0:T(8,128)S(1)}, f32[32,256]{1,0:T(8,128)S(1)}, u32[]{:S(2)}, u32[]{:S(2)}) collective-permute-start(f32[32,256]{1,0:T(8,128)S(1)} %convolution_add_fusion.15), channel_id=1, source_target_pairs={{64,0},{72,8},{80,16},{88,24},{96,32},{104,40},{112,48},{120,56},{... | collective-permute-start | bytes 98312 | tf_op jit(solution)/shard_map/ppermute | solution.py:12
  286.3 11.1 %collective-permute-start.20 = (f32[256,256]{1,0:T(8,128)S(1)}, f32[256,256]{1,0:T(8,128)S(1)}, u32[]{:S(2)}, u32[]{:S(2)}) collective-permute-start(f32[256,256]{1,0:T(8,128)S(1)} %fusion.61), channel_id=1, source_target_pairs={{64,0},{72,8},{80,16},{88,24},{96,32},{104,40},{112,48},{120,56},{... | collective-permute-start | bytes 786440 | tf_op jit(solution)/shard_map/ppermute | solution.py:12
  288.8 11.0 %collective-permute-start.19 = (f32[32,256]{1,0:T(8,128)S(1)}, f32[32,256]{1,0:T(8,128)S(1)}, u32[]{:S(2)}, u32[]{:S(2)}) collective-permute-start(f32[32,256]{1,0:T(8,128)S(1)} %convolution_add_fusion.14), channel_id=1, source_target_pairs={{128,0},{136,8},{144,16},{152,24},{160,32},{168,40},{176,48},{184,... | collective-permute-start | bytes 98312 | tf_op jit(solution)/shard_map/ppermute | solution.py:12
  297.8 17.0 %collective-permute-start.22 = (f32[256,256]{1,0:T(8,128)S(1)}, f32[256,256]{1,0:T(8,128)S(1)}, u32[]{:S(2)}, u32[]{:S(2)}) collective-permute-start(f32[256,256]{1,0:T(8,128)S(1)} %fusion.62), channel_id=1, source_target_pairs={{128,0},{136,8},{144,16},{152,24},{160,32},{168,40},{176,48},{184,... | collective-permute-start | bytes 786440 | tf_op jit(solution)/shard_map/ppermute | solution.py:12
  300.1 15.1 %collective-permute-start.21 = (f32[32,256]{1,0:T(8,128)S(1)}, f32[32,256]{1,0:T(8,128)S(1)}, u32[]{:S(2)}, u32[]{:S(2)}) collective-permute-start(f32[32,256]{1,0:T(8,128)S(1)} %convolution_add_fusion.13), channel_id=1, source_target_pairs={{256,0},{264,8},{272,16},{280,24},{288,32},{296,40},{304,48},{312,... | collective-permute-start | bytes 98312 | tf_op jit(solution)/shard_map/ppermute | solution.py:12
  315.6 7.1 collective-permute-start.23
  496.0 8.6 %collective-permute-start.24 = (f32[32,256]{1,0:T(8,128)S(1)}, f32[32,256]{1,0:T(8,128)S(1)}, u32[]{:S(2)}, u32[]{:S(2)}) collective-permute-start(f32[32,256]{1,0:T(8,128)S(1)} %get-tuple-element.574), channel_id=1, source_target_pairs={{0,8},{8,16},{16,24},{24,32},{32,40},{40,48},{48,56},{56,64},{64,7... | collective-permute-start | bytes 98312 | tf_op jit(solution)/shard_map/ppermute | solution.py:12
  504.9 9.1 %collective-permute-start.25 = (f32[32,256]{1,0:T(8,128)S(1)}, f32[32,256]{1,0:T(8,128)S(1)}, u32[]{:S(2)}, u32[]{:S(2)}) collective-permute-start(f32[32,256]{1,0:T(8,128)S(1)} %convolution_add_fusion.11), channel_id=1, source_target_pairs={{0,16},{8,24},{16,32},{24,40},{32,48},{40,56},{48,64},{56,72},{64,... | collective-permute-start | bytes 98312 | tf_op jit(solution)/shard_map/ppermute | solution.py:12
  514.4 9.6 %collective-permute-start.26 = (f32[32,256]{1,0:T(8,128)S(1)}, f32[32,256]{1,0:T(8,128)S(1)}, u32[]{:S(2)}, u32[]{:S(2)}) collective-permute-start(f32[32,256]{1,0:T(8,128)S(1)} %convolution_add_fusion.10), channel_id=1, source_target_pairs={{0,32},{8,40},{16,48},{24,56},{32,64},{40,72},{48,80},{56,88},{64,... | collective-permute-start | bytes 98312 | tf_op jit(solution)/shard_map/ppermute | solution.py:12
  524.3 7.0 collective-permute-start.27
  531.6 7.9 collective-permute-start.28
  539.9 9.7 %collective-permute-start.29 = (f32[32,256]{1,0:T(8,128)S(1)}, f32[32,256]{1,0:T(8,128)S(1)}, u32[]{:S(2)}, u32[]{:S(2)}) collective-permute-start(f32[32,256]{1,0:T(8,128)S(1)} %convolution_add_fusion.7), channel_id=1, source_target_pairs={{0,256},{8,264},{16,272},{24,280},{32,288},{40,296},{48,304},{56,3... | collective-permute-start | bytes 98312 | tf_op jit(solution)/shard_map/ppermute | solution.py:12
  550.0 8.6 %collective-permute-start.30 = (f32[32,256]{1,0:T(8,128)S(1)}, f32[32,256]{1,0:T(8,128)S(1)}, u32[]{:S(2)}, u32[]{:S(2)}) collective-permute-start(f32[32,256]{1,0:T(8,128)S(1)} %convolution_add_fusion.6), channel_id=1, source_target_pairs={{0,8},{8,16},{16,24},{24,32},{32,40},{40,48},{48,56},{56,64},{64,7... | collective-permute-start | bytes 98312 | tf_op jit(solution)/shard_map/ppermute | solution.py:12
  611.3 7.3 collective-permute-start.33
  635.6 17.8 %collective-permute-start.37 = (f32[32,256]{1,0:T(8,128)S(1)}, f32[32,256]{1,0:T(8,128)S(1)}, u32[]{:S(2)}, u32[]{:S(2)}) collective-permute-start(f32[32,256]{1,0:T(8,128)S(1)} %convolution_add_fusion), channel_id=1, source_target_pairs={{8,0},{16,8},{24,16},{32,24},{40,32},{48,40},{56,48},{64,56},{72,6... | collective-permute-start | bytes 98312 | tf_op jit(solution)/shard_map/ppermute | solution.py:12
  (10 other events, 192.9 us)
Sparse Core Ops, SparseCore 0:
  10.1 62.5 all-gather.1
where the time goes:
time: 818 us; the launch traced here: 812 us
  blocking collectives  258 us (32%)
  matrix products  221 us (27%)
  waiting for transfers between devices  214 us (26%)
  starting transfers between devices  95.2 us (12%)
  between operations  14.9 us (2%)
    dot_general x152, matrix products, transform(): lax.dot_general(vectors_in, matrix, (((1,), (1,)), ((), ())), precision=l...  175 us
    ppermute x38, waiting for transfers between devices, from_behind(): return lax.ppermute(block, axis, route)  148 us
    psum x1, blocking collectives, shards(): lax.psum(jnp.sum(second_solve * second_solve, axis=(0, 2)), 'chain')  129 us
    psum x1, blocking collectives, shards(): lax.psum(jnp.sum(first_solve * first_solve, axis=(0, 2)), 'chain')  129 us
    ppermute x38, starting transfers between devices, from_behind(): return lax.ppermute(block, axis, route)  95.2 us
    all_gather x1, waiting for transfers between devices, shards(): full_factors = lax.all_gather(factors, 'cols', axis=1, tiled=True)  64.7 us
    dot_general x42, matrix products, compose(): jnp.dot(later, earlier, precision=lax.Precision.HIGHEST, preferred_elemen...  46.4 us
  transfers between devices with their start and end apart: 39, of which 29 were waited for; matrix products, arithmetic and copies ran while one was open for 6% of the time, Pallas kernels for 0%

commit v1 on v0

--- a/solution.py
+++ b/solution.py
@@ -4,6 +4,12 @@
 from jax.sharding import PartitionSpec as P
 
 eps_value = 1e-06
+
+
+def add_all(block, axis):
+    parts = lax.all_gather(block, axis, axis=0, tiled=False)
+    summed = parts.sum(axis=0)
+    return summed
 
 
 def from_behind(block, axis, distance):
@@ -106,7 +112,7 @@
     second_solve = solve_system(
         full_factors, first_solve / scale_one[None, :, None], prefix_forward, prefix_backward
     )
-    second_squares = lax.psum(jnp.sum(second_solve * second_solve, axis=(0, 2)), "chain")
+    second_squares = add_all(jnp.sum(second_solve * second_solve, axis=(0, 2)), "chain")
     scale_two = jnp.sqrt(second_squares / cell_count + eps_value)
     result_vectors = second_solve / scale_two[None, :, None]
     return (result_vectors, jnp.log(scale_two))

time: 818 us -> 820 us (level)
    unnamed x0 -> x1, blocking collectives: none -> 131 us
    psum x1 -> x0, blocking collectives: 129 us -> none  [shards(): lax.psum(jnp.sum(second_solve * second_solve, axis=(0, 2)), 'chain')]
  transfers between devices with their start and end apart: 39 -> 39, of which waited for: 29 -> 28; matrix products, arithmetic and copies ran while one was open for 6% -> 6% of each run, Pallas kernels for 0% -> 0%
where the time goes in v1:
time: 820 us; the launch traced here: 815 us
  blocking collectives  260 us (32%)
  matrix products  221 us (27%)
  waiting for transfers between devices  212 us (26%)
  starting transfers between devices  95.2 us (12%)
  between operations  15.6 us (2%)
    dot_general x152, matrix products, transform(): lax.dot_general(vectors_in, matrix, (((1,), (1,)), ((), ())), precision=l...  175 us
    ppermute x38, waiting for transfers between devices, from_behind(): return lax.ppermute(block, axis, route)  147 us
    unnamed x1, blocking collectives  131 us
    psum x1, blocking collectives, shards(): lax.psum(jnp.sum(first_solve * first_solve, axis=(0, 2)), 'chain')  129 us
    ppermute x38, starting transfers between devices, from_behind(): return lax.ppermute(block, axis, route)  95.2 us
    all_gather x1, waiting for transfers between devices, shards(): full_factors = lax.all_gather(factors, 'cols', axis=1, tiled=True)  64.7 us
    dot_general x42, matrix products, compose(): jnp.dot(later, earlier, precision=lax.Precision.HIGHEST, preferred_elemen...  46.4 us
  transfers between devices with their start and end apart: 39, of which 28 were waited for; matrix products, arithmetic and copies ran while one was open for 6% of the time, Pallas kernels for 0%

profile of v1, /device:TPU:32, one launch (start us, length us, event | category | flops | bytes accessed | tf_op | source)
XLA Modules:
  0.0 814.8 jit_solution(15860850763824284428)
XLA Ops:
  8.0 64.7 %all-gather.3.cloned.1.call-done = f32[16,256,256]{2,1,0:T(8,128)} async-done(((f32[16,32,256]{2,1,0:T(8,128)}), f32[16,256,256]{2,1,0:T(8,128)}) %all-gather.3.cloned.1.call-update) | async-done | bytes 4194320 | tf_op jit(solution)/shard_map/all_gather | solution.py:87
  72.7 21.5 %while.146 = (s32[]{:T(128)}, f32[32,256]{1,0:T(8,128)S(1)}, f32[16,256,256]{2,1,0:T(8,128)}, f32[16,32,256]{2,1,0:T(8,128)}, s32[]{:T(128)}, /*index=5*/s32[]{:T(128)}) while((s32[]{:T(128)}, f32[32,256]{1,0:T(8,128)S(1)}, f32[16,256,256]{2,1,0:T(8,128)}, f32[16,32,256]{2,1,0:T(8,128)}, s32[]{:T(128)}, /*index=5*/s32[]{:T(128)}) %tuple.241), condition=%wide.region_1.2_spmd.clone, body=%wide.region_0.1_spmd.clone.sunk | while | flops 25182212 | bytes 427087 | solution.py:44
  96.1 22.1 %while.138 = (s32[]{:T(128)}, f32[256,256]{1,0:T(8,128)S(1)}, f32[16,256,256]{2,1,0:T(8,128)}, s32[]{:T(128)}) while((s32[]{:T(128)}, f32[256,256]{1,0:T(8,128)S(1)}, f32[16,256,256]{2,1,0:T(8,128)}, s32[]{:T(128)}) %tuple.273), condition=%wide.region_3.4_spmd, body=%wide.region_2.3_spmd.sunk | while | flops 201326592 | bytes 1311285 | solution.py:63
  134.6 7.3 collective-permute-done.4
  146.5 10.8 %collective-permute-done.6 = f32[256,256]{1,0:T(8,128)S(1)} collective-permute-done((f32[256,256]{1,0:T(8,128)S(1)}, f32[256,256]{1,0:T(8,128)S(1)}, u32[]{:S(2)}, u32[]{:S(2)}) %collective-permute-start.6) | collective-permute-done | bytes 262176 | tf_op jit(solution)/shard_map/ppermute | solution.py:18
  161.9 7.5 collective-permute-done.8
  173.3 7.5 collective-permute-done.10
  184.0 6.6 collective-permute-done.11
  190.7 21.4 %while.139 = (s32[]{:T(128)}, f32[32,256]{1,0:T(8,128)S(1)}, f32[16,32,256]{2,1,0:T(8,128)S(1)}, f32[16,256,256]{2,1,0:T(8,128)}, f32[16,32,256]{2,1,0:T(8,128)}, /*index=5*/s32[]{:T(128)}) while((s32[]{:T(128)}, f32[32,256]{1,0:T(8,128)S(1)}, f32[16,32,256]{2,1,0:T(8,128)S(1)}, f32[16,256,256]{2,1,0:T(8,128)}, f32[16,32,256]{2,1,0:T(8,128)}, ...), condition=%wide.region_5.6_spmd, body=%wide.region_4.5_spmd.sunk | while | flops 25174016 | bytes 459845 | solution.py:44
  212.2 21.3 %while.140 = (s32[]{:T(128)}, f32[32,256]{1,0:T(8,128)S(1)}, f32[16,32,256]{2,1,0:T(8,128)S(1)}, f32[16,256,256]{2,1,0:T(8,128)}, s32[]{:T(128)}, /*index=5*/s32[]{:T(128)}) while((s32[]{:T(128)}, f32[32,256]{1,0:T(8,128)S(1)}, f32[16,32,256]{2,1,0:T(8,128)S(1)}, f32[16,256,256]{2,1,0:T(8,128)}, s32[]{:T(128)}, /*index=5*/s32[]{:T(128)}) %tuple.275), condition=%wide.region_7.8_spmd, body=%wide.region_6.7_spmd.sunk | while | flops 25174020 | bytes 427089 | solution.py:54
  235.4 22.1 %while.141 = (s32[]{:T(128)}, f32[256,256]{1,0:T(8,128)S(1)}, f32[16,256,256]{2,1,0:T(8,128)}, s32[]{:T(128)}, s32[]{:T(128)}) while((s32[]{:T(128)}, f32[256,256]{1,0:T(8,128)S(1)}, f32[16,256,256]{2,1,0:T(8,128)}, s32[]{:T(128)}, s32[]{:T(128)}) %tuple.276), condition=%wide.region_9.10_spmd, body=%wide.region_8.9_spmd.sunk | while | flops 201326592 | bytes 1310797 | solution.py:63
  278.5 7.5 collective-permute-done.18
  290.8 6.7 collective-permute-done.20
  301.4 13.4 %collective-permute-done.22 = f32[256,256]{1,0:T(8,128)S(1)} collective-permute-done((f32[256,256]{1,0:T(8,128)S(1)}, f32[256,256]{1,0:T(8,128)S(1)}, u32[]{:S(2)}, u32[]{:S(2)}) %collective-permute-start.22) | collective-permute-done | bytes 262176 | tf_op jit(solution)/shard_map/ppermute | solution.py:18
  315.6 5.5 collective-permute-start.23
  322.7 21.6 %while.142 = (s32[]{:T(128)}, f32[32,256]{1,0:T(8,128)S(1)}, f32[16,32,256]{2,1,0:T(8,128)S(1)}, f32[16,32,256]{2,1,0:T(8,128)}, f32[16,256,256]{2,1,0:T(8,128)}, /*index=5*/s32[]{:T(128)}, s32[]{:T(128)}) while((s32[]{:T(128)}, f32[32,256]{1,0:T(8,128)S(1)}, f32[16,32,256]{2,1,0:T(8,128)S(1)}, f32[16,32,256]{2,1,0:T(8,128)}, ...), condition=%wide.region_11.12_spmd, body=%wide.region_10.11_spmd.sunk | while | flops 25174020 | bytes 460377 | solution.py:54
  344.5 129.1 %psum.7 = f32[32]{0:T(128)S(1)} all-reduce(f32[32]{0:T(128)S(1)} %multiply_reduce_fusion.1), channel_id=1, replica_groups=mesh['chain'=64,'cols'=8] {'chain'}, use_global_device_ids=true, to_apply=%region_13.14 | all-reduce | flops 32 | bytes 256 | tf_op jit(solution)/shard_map/psum | solution.py:110
  474.6 21.5 %while.147 = (s32[]{:T(128)}, f32[32,256]{1,0:T(8,128)S(1)}, f32[16,256,256]{2,1,0:T(8,128)}, f32[16,32,256]{2,1,0:T(8,128)}, s32[]{:T(128)}, /*index=5*/s32[]{:T(128)}) while((s32[]{:T(128)}, f32[32,256]{1,0:T(8,128)S(1)}, f32[16,256,256]{2,1,0:T(8,128)}, f32[16,32,256]{2,1,0:T(8,128)}, s32[]{:T(128)}, ...), condition=%wide.region_15.16_spmd.clone, body=%wide.region_14.15_spmd.clone.sunk | while | flops 25182212 | bytes 427087 | solution.py:44
  497.9 6.6 collective-permute-done.24
  506.9 7.2 collective-permute-done.25
  516.5 7.5 collective-permute-done.26
  526.2 5.1 collective-permute-done.27
  533.6 6.0 collective-permute-done.28
  541.4 8.2 %collective-permute-done.29 = f32[32,256]{1,0:T(8,128)S(1)} collective-permute-done((f32[32,256]{1,0:T(8,128)S(1)}, f32[32,256]{1,0:T(8,128)S(1)}, u32[]{:S(2)}, u32[]{:S(2)}) %collective-permute-start.29) | collective-permute-done | bytes 32800 | tf_op jit(solution)/shard_map/ppermute | solution.py:18
  551.9 6.6 collective-permute-done.30
  558.6 21.4 %while.143 = (s32[]{:T(128)}, f32[32,256]{1,0:T(8,128)S(1)}, f32[16,32,256]{2,1,0:T(8,128)S(1)}, f32[16,256,256]{2,1,0:T(8,128)}, f32[16,32,256]{2,1,0:T(8,128)}, /*index=5*/s32[]{:T(128)}) while((s32[]{:T(128)}, f32[32,256]{1,0:T(8,128)S(1)}, f32[16,32,256]{2,1,0:T(8,128)S(1)}, f32[16,256,256]{2,1,0:T(8,128)}, f32[16,32,256]{2,1,0:T(8,128)}, ...), condition=%wide.region_17.18_spmd, body=%wide.region_16.17_spmd.sunk | while | flops 25174016 | bytes 459845 | solution.py:44
  580.0 21.3 %while.144 = (s32[]{:T(128)}, f32[32,256]{1,0:T(8,128)S(1)}, f32[16,32,256]{2,1,0:T(8,128)S(1)}, f32[16,256,256]{2,1,0:T(8,128)}, s32[]{:T(128)}, /*index=5*/s32[]{:T(128)}) while((s32[]{:T(128)}, f32[32,256]{1,0:T(8,128)S(1)}, f32[16,32,256]{2,1,0:T(8,128)S(1)}, f32[16,256,256]{2,1,0:T(8,128)}, s32[]{:T(128)}, /*index=5*/s32[]{:T(128)}) %tuple.280), condition=%wide.region_19.20_spmd, body=%wide.region_18.19_spmd.sunk | while | flops 25174020 | bytes 427089 | solution.py:54
  613.3 5.4 collective-permute-done.33
  627.3 4.8 collective-permute-done.35
  635.7 16.2 %collective-permute-start.37 = (f32[32,256]{1,0:T(8,128)S(1)}, f32[32,256]{1,0:T(8,128)S(1)}, u32[]{:S(2)}, u32[]{:S(2)}) collective-permute-start(f32[32,256]{1,0:T(8,128)S(1)} %convolution_add_fusion), channel_id=1, source_target_pairs={{8,0},{16,8},{24,16},{32,24},{40,32},{48,40},{56,48},{64,56},{72,6... | collective-permute-start | bytes 98312 | tf_op jit(solution)/shard_map/ppermute | solution.py:18
  653.9 21.3 %while.145 = (s32[]{:T(128)}, f32[32,256]{1,0:T(8,128)S(1)}, f32[16,32,256]{2,1,0:T(8,128)S(1)}, f32[16,32,256]{2,1,0:T(8,128)S(1)}, f32[16,256,256]{2,1,0:T(8,128)}, /*index=5*/s32[]{:T(128)}, s32[]{:T(128)}) while((s32[]{:T(128)}, f32[32,256]{1,0:T(8,128)S(1)}, f32[16,32,256]{2,1,0:T(8,128)S(1)}, f32[16,32,256]{2,1,0:T(8,128)S(1)}, ...), condition=%wide.region_21.22_spmd, body=%wide.region_20.21_spmd.sunk | while | flops 25174020 | bytes 460377 | solution.py:54
  675.6 130.8 %all-reduce = f32[2048]{0:T(1024)S(1)} all-reduce(f32[2048]{0:T(1024)S(1)} %dynamic-update-slice), channel_id=2, replica_groups=mesh['chain'=64,'cols'=8] {'chain'}, use_global_device_ids=true, to_apply=%add | all-reduce | flops 2048 | bytes 16384
  (440 shorter events, 323.4 us)
Async XLA Ops:
  7.2 65.5 %all-gather.3.cloned.1.call-start = ((), (), s32[]{:S(2)}) async-start(), calls=%async_computation | async-start | bytes 4718592 | tf_op jit(solution)/shard_map/all_gather | solution.py:87
  94.1 27.5 %collective-permute-start = (f32[32,256]{1,0:T(8,128)S(1)}, f32[32,256]{1,0:T(8,128)S(1)}, u32[]{:S(2)}, u32[]{:S(2)}) collective-permute-start(f32[32,256]{1,0:T(8,128)S(1)} %get-tuple-element.568), channel_id=1, source_target_pairs={{0,8},{8,16},{16,24},{24,32},{32,40},{40,48},{48,56},{56,64},{64,7... | collective-permute-start | bytes 98312 | tf_op jit(solution)/shard_map/ppermute | solution.py:18
  118.2 11.0 %collective-permute-start.2 = (f32[256,256]{1,0:T(8,128)S(1)}, f32[256,256]{1,0:T(8,128)S(1)}, u32[]{:S(2)}, u32[]{:S(2)}) collective-permute-start(f32[256,256]{1,0:T(8,128)S(1)} %get-tuple-element.569), channel_id=1, source_target_pairs={{0,8},{8,16},{16,24},{24,32},{32,40},{40,48},{48,56},{56,64},{64,7... | collective-permute-start | bytes 786440 | tf_op jit(solution)/shard_map/ppermute | solution.py:18
  122.0 9.5 %collective-permute-start.1 = (f32[32,256]{1,0:T(8,128)S(1)}, f32[32,256]{1,0:T(8,128)S(1)}, u32[]{:S(2)}, u32[]{:S(2)}) collective-permute-start(f32[32,256]{1,0:T(8,128)S(1)} %convolution_add_fusion.23), channel_id=1, source_target_pairs={{0,16},{8,24},{16,32},{24,40},{32,48},{40,56},{48,64},{56,72},{64,... | collective-permute-start | bytes 98312 | tf_op jit(solution)/shard_map/ppermute | solution.py:18
  129.6 12.3 %collective-permute-start.4 = (f32[256,256]{1,0:T(8,128)S(1)}, f32[256,256]{1,0:T(8,128)S(1)}, u32[]{:S(2)}, u32[]{:S(2)}) collective-permute-start(f32[256,256]{1,0:T(8,128)S(1)} %fusion.54), channel_id=1, source_target_pairs={{0,16},{8,24},{16,32},{24,40},{32,48},{40,56},{48,64},{56,72},{64,... | collective-permute-start | bytes 786440 | tf_op jit(solution)/shard_map/ppermute | solution.py:18
  131.9 12.3 %collective-permute-start.3 = (f32[32,256]{1,0:T(8,128)S(1)}, f32[32,256]{1,0:T(8,128)S(1)}, u32[]{:S(2)}, u32[]{:S(2)}) collective-permute-start(f32[32,256]{1,0:T(8,128)S(1)} %convolution_add_fusion.22), channel_id=1, source_target_pairs={{0,32},{8,40},{16,48},{24,56},{32,64},{40,72},{48,80},{56,88},{64,... | collective-permute-start | bytes 98312 | tf_op jit(solution)/shard_map/ppermute | solution.py:18
  142.3 15.0 %collective-permute-start.6 = (f32[256,256]{1,0:T(8,128)S(1)}, f32[256,256]{1,0:T(8,128)S(1)}, u32[]{:S(2)}, u32[]{:S(2)}) collective-permute-start(f32[256,256]{1,0:T(8,128)S(1)} %fusion.55), channel_id=1, source_target_pairs={{0,32},{8,40},{16,48},{24,56},{32,64},{40,72},{48,80},{56,88},{64,... | collective-permute-start | bytes 786440 | tf_op jit(solution)/shard_map/ppermute | solution.py:18
  144.5 15.1 %collective-permute-start.5 = (f32[32,256]{1,0:T(8,128)S(1)}, f32[32,256]{1,0:T(8,128)S(1)}, u32[]{:S(2)}, u32[]{:S(2)}) collective-permute-start(f32[32,256]{1,0:T(8,128)S(1)} %convolution_add_fusion.21), channel_id=1, source_target_pairs={{0,64},{8,72},{16,80},{24,88},{32,96},{40,104},{48,112},{56,120},{... | collective-permute-start | bytes 98312 | tf_op jit(solution)/shard_map/ppermute | solution.py:18
  157.7 11.7 %collective-permute-start.8 = (f32[256,256]{1,0:T(8,128)S(1)}, f32[256,256]{1,0:T(8,128)S(1)}, u32[]{:S(2)}, u32[]{:S(2)}) collective-permute-start(f32[256,256]{1,0:T(8,128)S(1)} %fusion.56), channel_id=1, source_target_pairs={{0,64},{8,72},{16,80},{24,88},{32,96},{40,104},{48,112},{56,120},{... | collective-permute-start | bytes 786440 | tf_op jit(solution)/shard_map/ppermute | solution.py:18
  160.0 11.7 %collective-permute-start.7 = (f32[32,256]{1,0:T(8,128)S(1)}, f32[32,256]{1,0:T(8,128)S(1)}, u32[]{:S(2)}, u32[]{:S(2)}) collective-permute-start(f32[32,256]{1,0:T(8,128)S(1)} %convolution_add_fusion.20), channel_id=1, source_target_pairs={{0,128},{8,136},{16,144},{24,152},{32,160},{40,168},{48,176},{56,1... | collective-permute-start | bytes 98312 | tf_op jit(solution)/shard_map/ppermute | solution.py:18
  169.8 11.1 %collective-permute-start.10 = (f32[256,256]{1,0:T(8,128)S(1)}, f32[256,256]{1,0:T(8,128)S(1)}, u32[]{:S(2)}, u32[]{:S(2)}) collective-permute-start(f32[256,256]{1,0:T(8,128)S(1)} %fusion.57), channel_id=1, source_target_pairs={{0,128},{8,136},{16,144},{24,152},{32,160},{40,168},{48,176},{56,1... | collective-permute-start | bytes 786440 | tf_op jit(solution)/shard_map/ppermute | solution.py:18
  172.0 9.7 %collective-permute-start.9 = (f32[32,256]{1,0:T(8,128)S(1)}, f32[32,256]{1,0:T(8,128)S(1)}, u32[]{:S(2)}, u32[]{:S(2)}) collective-permute-start(f32[32,256]{1,0:T(8,128)S(1)} %convolution_add_fusion.19), channel_id=1, source_target_pairs={{0,256},{8,264},{16,272},{24,280},{32,288},{40,296},{48,304},{56,3... | collective-permute-start | bytes 98312 | tf_op jit(solution)/shard_map/ppermute | solution.py:18
  182.1 8.6 %collective-permute-start.11 = (f32[32,256]{1,0:T(8,128)S(1)}, f32[32,256]{1,0:T(8,128)S(1)}, u32[]{:S(2)}, u32[]{:S(2)}) collective-permute-start(f32[32,256]{1,0:T(8,128)S(1)} %convolution_add_fusion.18), channel_id=1, source_target_pairs={{0,8},{8,16},{16,24},{24,32},{32,40},{40,48},{48,56},{56,64},{64,7... | collective-permute-start | bytes 98312 | tf_op jit(solution)/shard_map/ppermute | solution.py:18
  233.5 26.0 %collective-permute-start.12 = (f32[32,256]{1,0:T(8,128)S(1)}, f32[32,256]{1,0:T(8,128)S(1)}, u32[]{:S(2)}, u32[]{:S(2)}) collective-permute-start(f32[32,256]{1,0:T(8,128)S(1)} %get-tuple-element.571), channel_id=1, source_target_pairs={{8,0},{16,8},{24,16},{32,24},{40,32},{48,40},{56,48},{64,56},{72,6... | collective-permute-start | bytes 98312 | tf_op jit(solution)/shard_map/ppermute | solution.py:18
  264.1 9.8 %collective-permute-start.16 = (f32[256,256]{1,0:T(8,128)S(1)}, f32[256,256]{1,0:T(8,128)S(1)}, u32[]{:S(2)}, u32[]{:S(2)}) collective-permute-start(f32[256,256]{1,0:T(8,128)S(1)} %fusion.59), channel_id=1, source_target_pairs={{16,0},{24,8},{32,16},{40,24},{48,32},{56,40},{64,48},{72,56},{80,... | collective-permute-start | bytes 786440 | tf_op jit(solution)/shard_map/ppermute | solution.py:18
  267.0 9.2 %collective-permute-start.15 = (f32[32,256]{1,0:T(8,128)S(1)}, f32[32,256]{1,0:T(8,128)S(1)}, u32[]{:S(2)}, u32[]{:S(2)}) collective-permute-start(f32[32,256]{1,0:T(8,128)S(1)} %convolution_add_fusion.16), channel_id=1, source_target_pairs={{32,0},{40,8},{48,16},{56,24},{64,32},{72,40},{80,48},{88,56},{96,... | collective-permute-start | bytes 98312 | tf_op jit(solution)/shard_map/ppermute | solution.py:18
  274.3 11.7 %collective-permute-start.18 = (f32[256,256]{1,0:T(8,128)S(1)}, f32[256,256]{1,0:T(8,128)S(1)}, u32[]{:S(2)}, u32[]{:S(2)}) collective-permute-start(f32[256,256]{1,0:T(8,128)S(1)} %fusion.60), channel_id=1, source_target_pairs={{32,0},{40,8},{48,16},{56,24},{64,32},{72,40},{80,48},{88,56},{96,... | collective-permute-start | bytes 786440 | tf_op jit(solution)/shard_map/ppermute | solution.py:18
  276.6 11.9 %collective-permute-start.17 = (f32[32,256]{1,0:T(8,128)S(1)}, f32[32,256]{1,0:T(8,128)S(1)}, u32[]{:S(2)}, u32[]{:S(2)}) collective-permute-start(f32[32,256]{1,0:T(8,128)S(1)} %convolution_add_fusion.15), channel_id=1, source_target_pairs={{64,0},{72,8},{80,16},{88,24},{96,32},{104,40},{112,48},{120,56},{... | collective-permute-start | bytes 98312 | tf_op jit(solution)/shard_map/ppermute | solution.py:18
  286.3 11.1 %collective-permute-start.20 = (f32[256,256]{1,0:T(8,128)S(1)}, f32[256,256]{1,0:T(8,128)S(1)}, u32[]{:S(2)}, u32[]{:S(2)}) collective-permute-start(f32[256,256]{1,0:T(8,128)S(1)} %fusion.61), channel_id=1, source_target_pairs={{64,0},{72,8},{80,16},{88,24},{96,32},{104,40},{112,48},{120,56},{... | collective-permute-start | bytes 786440 | tf_op jit(solution)/shard_map/ppermute | solution.py:18
  288.8 11.0 %collective-permute-start.19 = (f32[32,256]{1,0:T(8,128)S(1)}, f32[32,256]{1,0:T(8,128)S(1)}, u32[]{:S(2)}, u32[]{:S(2)}) collective-permute-start(f32[32,256]{1,0:T(8,128)S(1)} %convolution_add_fusion.14), channel_id=1, source_target_pairs={{128,0},{136,8},{144,16},{152,24},{160,32},{168,40},{176,48},{184,... | collective-permute-start | bytes 98312 | tf_op jit(solution)/shard_map/ppermute | solution.py:18
  297.8 17.0 %collective-permute-start.22 = (f32[256,256]{1,0:T(8,128)S(1)}, f32[256,256]{1,0:T(8,128)S(1)}, u32[]{:S(2)}, u32[]{:S(2)}) collective-permute-start(f32[256,256]{1,0:T(8,128)S(1)} %fusion.62), channel_id=1, source_target_pairs={{128,0},{136,8},{144,16},{152,24},{160,32},{168,40},{176,48},{184,... | collective-permute-start | bytes 786440 | tf_op jit(solution)/shard_map/ppermute | solution.py:18
  300.1 15.1 %collective-permute-start.21 = (f32[32,256]{1,0:T(8,128)S(1)}, f32[32,256]{1,0:T(8,128)S(1)}, u32[]{:S(2)}, u32[]{:S(2)}) collective-permute-start(f32[32,256]{1,0:T(8,128)S(1)} %convolution_add_fusion.13), channel_id=1, source_target_pairs={{256,0},{264,8},{272,16},{280,24},{288,32},{296,40},{304,48},{312,... | collective-permute-start | bytes 98312 | tf_op jit(solution)/shard_map/ppermute | solution.py:18
  315.6 7.1 collective-permute-start.23
  496.0 8.6 %collective-permute-start.24 = (f32[32,256]{1,0:T(8,128)S(1)}, f32[32,256]{1,0:T(8,128)S(1)}, u32[]{:S(2)}, u32[]{:S(2)}) collective-permute-start(f32[32,256]{1,0:T(8,128)S(1)} %get-tuple-element.574), channel_id=1, source_target_pairs={{0,8},{8,16},{16,24},{24,32},{32,40},{40,48},{48,56},{56,64},{64,7... | collective-permute-start | bytes 98312 | tf_op jit(solution)/shard_map/ppermute | solution.py:18
  504.9 9.1 %collective-permute-start.25 = (f32[32,256]{1,0:T(8,128)S(1)}, f32[32,256]{1,0:T(8,128)S(1)}, u32[]{:S(2)}, u32[]{:S(2)}) collective-permute-start(f32[32,256]{1,0:T(8,128)S(1)} %convolution_add_fusion.11), channel_id=1, source_target_pairs={{0,16},{8,24},{16,32},{24,40},{32,48},{40,56},{48,64},{56,72},{64,... | collective-permute-start | bytes 98312 | tf_op jit(solution)/shard_map/ppermute | solution.py:18
  514.4 9.6 %collective-permute-start.26 = (f32[32,256]{1,0:T(8,128)S(1)}, f32[32,256]{1,0:T(8,128)S(1)}, u32[]{:S(2)}, u32[]{:S(2)}) collective-permute-start(f32[32,256]{1,0:T(8,128)S(1)} %convolution_add_fusion.10), channel_id=1, source_target_pairs={{0,32},{8,40},{16,48},{24,56},{32,64},{40,72},{48,80},{56,88},{64,... | collective-permute-start | bytes 98312 | tf_op jit(solution)/shard_map/ppermute | solution.py:18
  524.3 7.0 collective-permute-start.27
  531.7 7.9 collective-permute-start.28
  539.9 9.7 %collective-permute-start.29 = (f32[32,256]{1,0:T(8,128)S(1)}, f32[32,256]{1,0:T(8,128)S(1)}, u32[]{:S(2)}, u32[]{:S(2)}) collective-permute-start(f32[32,256]{1,0:T(8,128)S(1)} %convolution_add_fusion.7), channel_id=1, source_target_pairs={{0,256},{8,264},{16,272},{24,280},{32,288},{40,296},{48,304},{56,3... | collective-permute-start | bytes 98312 | tf_op jit(solution)/shard_map/ppermute | solution.py:18
  550.0 8.6 %collective-permute-start.30 = (f32[32,256]{1,0:T(8,128)S(1)}, f32[32,256]{1,0:T(8,128)S(1)}, u32[]{:S(2)}, u32[]{:S(2)}) collective-permute-start(f32[32,256]{1,0:T(8,128)S(1)} %convolution_add_fusion.6), channel_id=1, source_target_pairs={{0,8},{8,16},{16,24},{24,32},{32,40},{40,48},{48,56},{56,64},{64,7... | collective-permute-start | bytes 98312 | tf_op jit(solution)/shard_map/ppermute | solution.py:18
  611.4 7.3 collective-permute-start.33
  635.7 18.2 %collective-permute-start.37 = (f32[32,256]{1,0:T(8,128)S(1)}, f32[32,256]{1,0:T(8,128)S(1)}, u32[]{:S(2)}, u32[]{:S(2)}) collective-permute-start(f32[32,256]{1,0:T(8,128)S(1)} %convolution_add_fusion), channel_id=1, source_target_pairs={{8,0},{16,8},{24,16},{32,24},{40,32},{48,40},{56,48},{64,56},{72,6... | collective-permute-start | bytes 98312 | tf_op jit(solution)/shard_map/ppermute | solution.py:18
  (10 other events, 192.9 us)
Sparse Core Ops, SparseCore 0:
  10.1 62.5 all-gather.2
